TPU v7x, 128 devices: a whole 4x4x4 slice. The times are simulated.
128 devices in a mesh: row: 16 (over z_hi, y, core), col: 8 (over x, z_lo).
Axes of the slice: x: 4, y: 4, z: 4 (z_hi: 2, z_lo: 2; z = z_hi * 2 + z_lo), core: 2. Of those that a mesh axis runs over, the one named last changes fastest.
Arguments:
- word_topic: bfloat16 [131072, 128], P(('row', 'col')), may hold values from 0.25 to 4
- topic_weight: float32 [128], replicated, may hold values from 0.1 to 10
- tile_blocks: int32 [16, 8, 64, 2], P('row', 'col'), may hold values from 0 to 63, as said below
- tile_live: int32 [16, 8], P('row', 'col'), may hold values from 16 to 64, as said below
- pair_counts: int32 [16, 8, 64, 256, 256], P('row', 'col'), may hold values from 0 to 63
Outputs:
- next_word_topic: bfloat16 [131072, 128], P(('row', 'col'))
- next_topic_weight: float32 [128], replicated
Inputs may be any that keep to these rules, and one draw needn't show every extreme that they name: `tile_blocks`: each entry pair is (a word block among the device's 32 blocks of first words, a word block among its 64 blocks of second words); the slots of one device name distinct tiles. `tile_live`: slots at or beyond a device's count hold no tile; some device fills all slots.
All inputs are finite; a program needn't handle non-finite values.
Results may differ from a plain program's by a relative error of at most 0.0049.
Values may be sent and summed in bfloat16 or wider, within the bound.
No kernel may reach another device: no remote copies, remote signals or barrier semaphores. Data moves between devices by JAX's collectives and lax.ppermute only.
A program may use at most 128 MiB of HBM per device.

v0:
```python
from functools import partial
import jax
import jax.numpy as jnp
from jax import lax
from jax.sharding import PartitionSpec as P

V = 131072
K = 128
BLK = 256
ITERS = 2


def group_step(
    left_blocks, right_blocks, blocks, tiles_all, live, want_row, want_col, group, carry
):
    tile_group = 8
    start = group * tile_group
    row_ids = lax.dynamic_slice_in_dim(blocks[:, 0], start, tile_group)
    col_ids = lax.dynamic_slice_in_dim(blocks[:, 1], start, tile_group)
    tiles = lax.dynamic_slice_in_dim(tiles_all, start, tile_group, 0)
    alive = start + jnp.arange(tile_group, dtype=jnp.int32) < live
    left = left_blocks[row_ids]
    right = right_blocks[col_ids]
    denoms = jnp.einsum("gak,gbk->gab", left, right, preferred_element_type=jnp.float32)
    ratio = jnp.where(alive[:, None, None], tiles.astype(jnp.float32) / denoms, 0.0).astype(
        jnp.bfloat16
    )
    results = []
    place = 0
    row_part = jnp.einsum("gab,gbk->gak", ratio, right, preferred_element_type=jnp.float32)
    results.append(carry[place].at[row_ids].add(row_part))
    place = place + 1
    col_part = jnp.einsum("gab,gak->gbk", ratio, left, preferred_element_type=jnp.float32)
    results.append(carry[place].at[col_ids].add(col_part))
    return tuple(results)


def sweep(left_blocks, right_blocks, blocks, tiles_all, live):
    starts = []
    starts.append(jnp.zeros(left_blocks.shape, jnp.float32))
    starts.append(jnp.zeros(right_blocks.shape, jnp.float32))
    stepper = partial(group_step, left_blocks, right_blocks, blocks, tiles_all, live, True, True)
    turns = (live + 7) // 8
    return lax.fori_loop(0, turns, stepper, tuple(starts))


def local(word_topic, topic_weight, tile_blocks, tile_live, pair_counts):
    blocks = tile_blocks[0, 0]
    live = tile_live[0, 0]
    tiles_all = pair_counts[0, 0]
    weights = word_topic
    shares = topic_weight
    for step in range(ITERS):
        row_phi = lax.all_gather(weights, "col", axis=0, tiled=True)
        col_phi = lax.all_gather(weights, "row", axis=0, tiled=True)
        scaled = (row_phi.astype(jnp.float32) * shares).astype(jnp.bfloat16)
        left_blocks = scaled.reshape(-1, BLK, K)
        right_blocks = col_phi.reshape(-1, BLK, K)
        row_acc, col_acc = sweep(left_blocks, right_blocks, blocks, tiles_all, live)
        row_terms = row_acc.reshape(-1, K)
        col_terms = col_acc.reshape(-1, K)
        row_sum = lax.psum_scatter(row_terms, "col", scatter_dimension=0, tiled=True)
        col_sum = lax.psum_scatter(col_terms, "row", scatter_dimension=0, tiled=True)
        expected = weights.astype(jnp.float32) * (shares * row_sum + col_sum)
        totals = lax.psum(jnp.sum(expected, axis=0), ("row", "col"))
        weights = (V * expected / totals).astype(jnp.bfloat16)
        shares = K * totals / jnp.sum(totals)
    return (weights, shares)


def solution(mesh):
    in_specs = (
        P(("row", "col"), None),
        P(),
        P("row", "col", None, None),
        P("row", "col"),
        P("row", "col", None, None, None),
    )
    out_specs = (P(("row", "col"), None), P())
    return jax.shard_map(local, mesh=mesh, in_specs=in_specs, out_specs=out_specs, check_vma=False)
```

profile of v0, /device:TPU:1, one launch (start us, length us, event | category | flops | bytes accessed | tf_op | source)
XLA Modules:
  0.0 1029.4 jit_solution(16607636807630387287)
XLA Ops:
  9.4 52.8 %all-gather.5.cloned.1.call-done = bf16[8192,128]{1,0:T(8,128)(2,1)} async-done(((bf16[1024,128]{1,0:T(8,128)(2,1)}), bf16[8192,128]{1,0:T(8,128)(2,1)}) %all-gather.5.cloned.1.call-update) | async-done | bytes 2097168 | tf_op jit(solution)/shard_map/all_gather | solution.py:54
  65.5 57.8 %all-gather.7.cloned.1.call-done = bf16[16384,128]{1,0:T(8,128)(2,1)} async-done(((bf16[1024,128]{1,0:T(8,128)(2,1)}), bf16[16384,128]{1,0:T(8,128)(2,1)}) %all-gather.7.cloned.1.call-update) | async-done | bytes 4194320 | tf_op jit(solution)/shard_map/all_gather | solution.py:55
  123.3 4.2 broadcast.60.clone
  130.0 108.6 %while.24 = (s32[]{:T(128)}, f32[32,256,128]{2,1,0:T(8,128)}, f32[64,256,128]{2,1,0:T(8,128)}, s32[]{:T(128)}, s32[64,2]{0,1:T(2,128)S(1)}, /*index=5*/s32[]{:T(...) while((s32[]{:T(128)}, f32[32,256,128]{2,1,0:T(8,128)}, ...), condition=%wide.region_3.4_spmd, body=%wide.region_0.3_spmd.sunk | while | flops 405276736 | bytes 17835532 | solution.py:44
  138.4 3.4 scatter_fusion.1
  185.0 3.4 scatter_fusion.1
  216.0 3.4 scatter_fusion.1
  231.5 3.4 scatter_fusion.1
  235.3 3.4 scatter_fusion
  239.3 103.5 %reduce-scatter.5.cloned.1.call-done = f32[1024,128]{1,0:T(8,128)} async-done(((f32[8192,128]{1,0:T(8,128)}), f32[1024,128]{1,0:T(8,128)}) %reduce-scatter.5.cloned.1.call-update) | async-done | bytes 524304 | tf_op jit(solution)/shard_map/reduce_scatter | solution.py:62
  342.8 106.7 %reduce-scatter.7.cloned.1.call-done = f32[1024,128]{1,0:T(8,128)} async-done(((f32[16384,128]{1,0:T(8,128)}), f32[1024,128]{1,0:T(8,128)}) %reduce-scatter.7.cloned.1.call-update) | async-done | bytes 524304 | tf_op jit(solution)/shard_map/reduce_scatter | solution.py:63
  450.9 65.3 %psum.14 = f32[128]{0:T(128)S(1)} all-reduce(f32[128]{0:T(128)S(1)} %fusion.4), channel_id=1, replica_groups=mesh['row'=16,'col'=8] {'row','col'}, use_global_device_ids=true, to_apply=%region_7.8 | all-reduce | flops 128 | bytes 1024 | tf_op jit(solution)/shard_map/psum | solution.py:65
  520.1 43.9 %all-gather.9.cloned.1.call-done = bf16[8192,128]{1,0:T(8,128)(2,1)} async-done(((bf16[1024,128]{1,0:T(8,128)(2,1)}), bf16[8192,128]{1,0:T(8,128)(2,1)}) %all-gather.9.cloned.1.call-update) | async-done | bytes 2097168 | tf_op jit(solution)/shard_map/all_gather | solution.py:54
  567.4 58.3 %all-gather.11.cloned.1.call-done = bf16[16384,128]{1,0:T(8,128)(2,1)} async-done(((bf16[1024,128]{1,0:T(8,128)(2,1)}), bf16[16384,128]{1,0:T(8,128)(2,1)}) %all-gather.11.cloned.1.call-update) | async-done | bytes 4194320 | tf_op jit(solution)/shard_map/all_gather | solution.py:55
  625.7 4.2 broadcast.60
  632.4 108.6 %while.25 = (s32[]{:T(128)}, f32[32,256,128]{2,1,0:T(8,128)}, f32[64,256,128]{2,1,0:T(8,128)}, s32[]{:T(128)}, s32[64,2]{0,1:T(2,128)S(1)}, /*index=5*/s32[]{:T(...) while((s32[]{:T(128)}, f32[32,256,128]{2,1,0:T(8,128)}, ...), condition=%wide.region_12.13_spmd, body=%wide.region_9.12_spmd.sunk | while | flops 405276736 | bytes 17835532 | solution.py:44
  640.8 3.4 scatter_fusion.3
  687.4 3.4 scatter_fusion.3
  718.4 3.4 scatter_fusion.3
  733.9 3.4 scatter_fusion.3
  737.7 3.4 scatter_fusion.2
  741.8 103.4 %reduce-scatter.9.cloned.1.call-done = f32[1024,128]{1,0:T(8,128)} async-done(((f32[8192,128]{1,0:T(8,128)}), f32[1024,128]{1,0:T(8,128)}) %reduce-scatter.9.cloned.1.call-update) | async-done | bytes 524304 | tf_op jit(solution)/shard_map/reduce_scatter | solution.py:62
  845.2 106.7 %reduce-scatter.11.cloned.1.call-done = f32[1024,128]{1,0:T(8,128)} async-done(((f32[16384,128]{1,0:T(8,128)}), f32[1024,128]{1,0:T(8,128)}) %reduce-scatter.11.cloned.1.call-update) | async-done | bytes 524304 | tf_op jit(solution)/shard_map/reduce_scatter | solution.py:63
  953.2 65.5 %psum.15 = f32[128]{0:T(128)S(1)} all-reduce(f32[128]{0:T(128)S(1)} %fusion.5), channel_id=1, replica_groups=mesh['row'=16,'col'=8] {'row','col'}, use_global_device_ids=true, to_apply=%region_16.17 | all-reduce | flops 128 | bytes 1024 | tf_op jit(solution)/shard_map/psum | solution.py:65
  (194 shorter events, 207.6 us)
Async XLA Ops:
  7.2 55.0 %all-gather.5.cloned.1.call-start = ((), (), s32[]{:S(2)}) async-start(), calls=%async_computation.4 | async-start | bytes 2359296 | tf_op jit(solution)/shard_map/all_gather | solution.py:54
  7.9 115.4 %all-gather.7.cloned.1.call-start = ((), (), s32[]{:S(2)}) async-start(), calls=%async_computation.5 | async-start | bytes 4456448 | tf_op jit(solution)/shard_map/all_gather | solution.py:55
  8.6 334.2 %reduce-scatter.5.cloned.1.call-start = ((), (), s32[]{:S(2)}) async-start(), calls=%async_computation.6 | async-start | bytes 4718592 | tf_op jit(solution)/shard_map/reduce_scatter | solution.py:62
  127.6 2.5 copy-start.2
  238.7 210.9 %reduce-scatter.7.cloned.1.call-start = ((), (), s32[]{:S(2)}) async-start(), calls=%async_computation.7 | async-start | bytes 8912896 | tf_op jit(solution)/shard_map/reduce_scatter | solution.py:63
  238.7 210.8 %copy-start.1 = (bf16[1024,128]{1,0:T(8,128)(2,1)S(1)}, bf16[1024,128]{1,0:T(8,128)(2,1)}, u32[]{:S(2)}) copy-start(bf16[1024,128]{1,0:T(8,128)(2,1)} %param.9) | copy-start | bytes 786436
  238.7 210.8 %copy-start.3 = (f32[128]{0:T(128)S(1)}, f32[128]{0:T(128)}, u32[]{:S(2)}) copy-start(f32[128]{0:T(128)} %param.10) | copy-start | bytes 1540
  239.3 324.8 %all-gather.9.cloned.1.call-start = ((), (), s32[]{:S(2)}) async-start(), calls=%async_computation.8 | async-start | bytes 2359296 | tf_op jit(solution)/shard_map/all_gather | solution.py:54
  518.2 107.5 %all-gather.11.cloned.1.call-start = ((), (), s32[]{:S(2)}) async-start(), calls=%async_computation.9 | async-start | bytes 4456448 | tf_op jit(solution)/shard_map/all_gather | solution.py:55
  518.8 326.4 %reduce-scatter.9.cloned.1.call-start = ((), (), s32[]{:S(2)}) async-start(), calls=%async_computation.10 | async-start | bytes 4718592 | tf_op jit(solution)/shard_map/reduce_scatter | solution.py:62
  741.0 210.8 %reduce-scatter.11.cloned.1.call-start = ((), (), s32[]{:S(2)}) async-start(), calls=%async_computation.11 | async-start | bytes 8912896 | tf_op jit(solution)/shard_map/reduce_scatter | solution.py:63
  741.1 210.8 %copy-start = (bf16[1024,128]{1,0:T(8,128)(2,1)S(1)}, bf16[1024,128]{1,0:T(8,128)(2,1)}, u32[]{:S(2)}) copy-start(bf16[1024,128]{1,0:T(8,128)(2,1)} %divide_convert_fusion.1) | copy-start | bytes 786436
Sparse Core Ops, SparseCore 0:
  9.6 52.4 all-gather.4
  64.6 58.7 all-gather.6
  238.8 103.9 reduce-scatter.4
  347.0 102.4 reduce-scatter.6
  518.3 45.6 all-gather.8
  566.9 58.7 all-gather.10
  741.2 103.9 reduce-scatter.8
  849.5 102.2 reduce-scatter.10
where the time goes:
time: 1030 us
  waiting for transfers between devices  636 us (62%)
  blocking collectives  131 us (13%)
  other arithmetic  120 us (12%)
  local copies, waits for them, and re-layouts  84.5 us (8%)
  matrix products  41.8 us (4%)
  between operations  14.8 us (1%)
    reduce_scatter x2, waiting for transfers between devices, local(): lax.psum_scatter(col_terms, 'row', scatter_dimension=0, tiled=True)  213 us
    reduce_scatter x2, waiting for transfers between devices, local(): lax.psum_scatter(row_terms, 'col', scatter_dimension=0, tiled=True)  207 us
    psum x2, blocking collectives, local(): totals = lax.psum(jnp.sum(expected, axis=0), ('row', 'col'))  131 us
    all_gather x2, waiting for transfers between devices, local(): col_phi = lax.all_gather(weights, 'row', axis=0, tiled=True)  116 us
    all_gather x2, waiting for transfers between devices, local(): row_phi = lax.all_gather(weights, 'col', axis=0, tiled=True)  96.7 us
    scatter-add x14, other arithmetic, group_step(): results.append(carry[place].at[col_ids].add(col_part))  46.9 us
    scatter-add x14, other arithmetic, group_step(): results.append(carry[place].at[row_ids].add(row_part))  46.4 us
    gather x14, local copies, waits for them, and re-layouts, group_step(): right = right_blocks[col_ids]  39.7 us
  transfers between devices with their start and end apart: 8, of which 8 were waited for; matrix products, arithmetic and copies ran while one was open for 1% of the time, Pallas kernels for 0%

commit v1 on v0

--- a/solution.py
+++ b/solution.py
@@ -62,7 +62,10 @@
         row_sum = lax.psum_scatter(row_terms, "col", scatter_dimension=0, tiled=True)
         col_sum = lax.psum_scatter(col_terms, "row", scatter_dimension=0, tiled=True)
         expected = weights.astype(jnp.float32) * (shares * row_sum + col_sum)
-        totals = lax.psum(jnp.sum(expected, axis=0), ("row", "col"))
+        draw_the_seats_all = lambda my_data, mesh_ax, axis_key: lax.psum(
+            lax.psum(my_data, axis_name=mesh_ax), axis_name=axis_key
+        )
+        totals = draw_the_seats_all(jnp.sum(expected, axis=0), "row", "col")
         weights = (V * expected / totals).astype(jnp.bfloat16)
         shares = K * totals / jnp.sum(totals)
     return (weights, shares)

time: 1030 us -> 1010 us (0.981)
  blocking collectives: 131 us -> 98.6 us
    psum x2 -> x4, blocking collectives: 131 us -> 98.6 us  [the longest x2 68.7 us: local(): lax.psum(my_data, axis_name=mesh_ax)]
where the time goes in v1:
time: 1010 us; the launch traced here: 1000 us
  waiting for transfers between devices  640 us (63%)
  other arithmetic  120 us (12%)
  blocking collectives  98.6 us (10%)
  local copies, waits for them, and re-layouts  84.5 us (8%)
  matrix products  41.8 us (4%)
  between operations  14.8 us (1%)
    reduce_scatter x2, waiting for transfers between devices, local(): lax.psum_scatter(col_terms, 'row', scatter_dimension=0, tiled=True)  213 us
    reduce_scatter x2, waiting for transfers between devices, local(): lax.psum_scatter(row_terms, 'col', scatter_dimension=0, tiled=True)  207 us
    all_gather x2, waiting for transfers between devices, local(): col_phi = lax.all_gather(weights, 'row', axis=0, tiled=True)  116 us
    all_gather x2, waiting for transfers between devices, local(): row_phi = lax.all_gather(weights, 'col', axis=0, tiled=True)  101 us
    psum x2, blocking collectives, local(): lax.psum(my_data, axis_name=mesh_ax)  68.7 us
    scatter-add x14, other arithmetic, group_step(): results.append(carry[place].at[col_ids].add(col_part))  46.9 us
    scatter-add x14, other arithmetic, group_step(): results.append(carry[place].at[row_ids].add(row_part))  46.4 us
    gather x14, local copies, waits for them, and re-layouts, group_step(): right = right_blocks[col_ids]  39.7 us
  transfers between devices with their start and end apart: 8, of which 8 were waited for; matrix products, arithmetic and copies ran while one was open for 1% of the time, Pallas kernels for 0%

profile of v1, /device:TPU:1, one launch (start us, length us, event | category | flops | bytes accessed | tf_op | source)
XLA Modules:
  0.0 1001.1 jit_solution(5540350984035442466)
XLA Ops:
  9.4 52.8 %all-gather.5.cloned.1.call-done = bf16[8192,128]{1,0:T(8,128)(2,1)} async-done(((bf16[1024,128]{1,0:T(8,128)(2,1)}), bf16[8192,128]{1,0:T(8,128)(2,1)}) %all-gather.5.cloned.1.call-update) | async-done | bytes 2097168 | tf_op jit(solution)/shard_map/all_gather | solution.py:54
  65.5 57.8 %all-gather.7.cloned.1.call-done = bf16[16384,128]{1,0:T(8,128)(2,1)} async-done(((bf16[1024,128]{1,0:T(8,128)(2,1)}), bf16[16384,128]{1,0:T(8,128)(2,1)}) %all-gather.7.cloned.1.call-update) | async-done | bytes 4194320 | tf_op jit(solution)/shard_map/all_gather | solution.py:55
  123.3 4.2 broadcast.60.clone
  130.0 108.6 %while.24 = (s32[]{:T(128)}, f32[32,256,128]{2,1,0:T(8,128)}, f32[64,256,128]{2,1,0:T(8,128)}, s32[]{:T(128)}, s32[64,2]{0,1:T(2,128)S(1)}, /*index=5*/s32[]{:T(...) while((s32[]{:T(128)}, f32[32,256,128]{2,1,0:T(8,128)}, ...), condition=%wide.region_3.4_spmd, body=%wide.region_0.3_spmd.sunk | while | flops 405276736 | bytes 17835532 | solution.py:44
  138.4 3.4 scatter_fusion.1
  185.0 3.4 scatter_fusion.1
  216.0 3.4 scatter_fusion.1
  231.5 3.4 scatter_fusion.1
  235.3 3.4 scatter_fusion
  239.3 103.5 %reduce-scatter.5.cloned.1.call-done = f32[1024,128]{1,0:T(8,128)} async-done(((f32[8192,128]{1,0:T(8,128)}), f32[1024,128]{1,0:T(8,128)}) %reduce-scatter.5.cloned.1.call-update) | async-done | bytes 524304 | tf_op jit(solution)/shard_map/reduce_scatter | solution.py:62
  342.8 106.7 %reduce-scatter.7.cloned.1.call-done = f32[1024,128]{1,0:T(8,128)} async-done(((f32[16384,128]{1,0:T(8,128)}), f32[1024,128]{1,0:T(8,128)}) %reduce-scatter.7.cloned.1.call-update) | async-done | bytes 524304 | tf_op jit(solution)/shard_map/reduce_scatter | solution.py:63
  450.9 34.2 %psum.28 = f32[128]{0:T(128)S(1)} all-reduce(f32[128]{0:T(128)S(1)} %fusion.4), channel_id=1, replica_groups=mesh['row'=16,'col'=8] {'row'}, use_global_device_ids=true, to_apply=%region_7.8 | all-reduce | flops 128 | bytes 1024 | tf_op jit(solution)/shard_map/psum | solution.py:66
  485.1 15.0 %psum.29 = f32[128]{0:T(128)S(1)} all-reduce(f32[128]{0:T(128)S(1)} %psum.28), channel_id=1, replica_groups=mesh['row'=16,'col'=8] {'col'}, use_global_device_ids=true, to_apply=%region_8.9 | all-reduce | flops 128 | bytes 1024 | tf_op jit(solution)/shard_map/psum | solution.py:65
  504.1 47.8 %all-gather.9.cloned.1.call-done = bf16[8192,128]{1,0:T(8,128)(2,1)} async-done(((bf16[1024,128]{1,0:T(8,128)(2,1)}), bf16[8192,128]{1,0:T(8,128)(2,1)}) %all-gather.9.cloned.1.call-update) | async-done | bytes 2097168 | tf_op jit(solution)/shard_map/all_gather | solution.py:54
  555.2 58.3 %all-gather.11.cloned.1.call-done = bf16[16384,128]{1,0:T(8,128)(2,1)} async-done(((bf16[1024,128]{1,0:T(8,128)(2,1)}), bf16[16384,128]{1,0:T(8,128)(2,1)}) %all-gather.11.cloned.1.call-update) | async-done | bytes 4194320 | tf_op jit(solution)/shard_map/all_gather | solution.py:55
  613.5 4.2 broadcast.60
  620.2 108.6 %while.25 = (s32[]{:T(128)}, f32[32,256,128]{2,1,0:T(8,128)}, f32[64,256,128]{2,1,0:T(8,128)}, s32[]{:T(128)}, s32[64,2]{0,1:T(2,128)S(1)}, /*index=5*/s32[]{:T(...) while((s32[]{:T(128)}, f32[32,256,128]{2,1,0:T(8,128)}, ...), condition=%wide.region_13.14_spmd, body=%wide.region_10.13_spmd.sunk | while | flops 405276736 | bytes 17835532 | solution.py:44
  628.6 3.4 scatter_fusion.3
  706.2 3.4 scatter_fusion.3
  721.7 3.4 scatter_fusion.3
  729.6 103.4 %reduce-scatter.9.cloned.1.call-done = f32[1024,128]{1,0:T(8,128)} async-done(((f32[8192,128]{1,0:T(8,128)}), f32[1024,128]{1,0:T(8,128)}) %reduce-scatter.9.cloned.1.call-update) | async-done | bytes 524304 | tf_op jit(solution)/shard_map/reduce_scatter | solution.py:62
  833.0 106.7 %reduce-scatter.11.cloned.1.call-done = f32[1024,128]{1,0:T(8,128)} async-done(((f32[16384,128]{1,0:T(8,128)}), f32[1024,128]{1,0:T(8,128)}) %reduce-scatter.11.cloned.1.call-update) | async-done | bytes 524304 | tf_op jit(solution)/shard_map/reduce_scatter | solution.py:63
  941.0 34.5 %psum.30 = f32[128]{0:T(128)S(1)} all-reduce(f32[128]{0:T(128)S(1)} %fusion.5), channel_id=1, replica_groups=mesh['row'=16,'col'=8] {'row'}, use_global_device_ids=true, to_apply=%region_17.18 | all-reduce | flops 128 | bytes 1024 | tf_op jit(solution)/shard_map/psum | solution.py:66
  975.5 14.9 %psum.31 = f32[128]{0:T(128)S(1)} all-reduce(f32[128]{0:T(128)S(1)} %psum.30), channel_id=1, replica_groups=mesh['row'=16,'col'=8] {'col'}, use_global_device_ids=true, to_apply=%region_18.19 | all-reduce | flops 128 | bytes 1024 | tf_op jit(solution)/shard_map/psum | solution.py:65
  (196 shorter events, 214.3 us)
Async XLA Ops:
  7.2 55.0 %all-gather.5.cloned.1.call-start = ((), (), s32[]{:S(2)}) async-start(), calls=%async_computation.4 | async-start | bytes 2359296 | tf_op jit(solution)/shard_map/all_gather | solution.py:54
  7.9 115.4 %all-gather.7.cloned.1.call-start = ((), (), s32[]{:S(2)}) async-start(), calls=%async_computation.5 | async-start | bytes 4456448 | tf_op jit(solution)/shard_map/all_gather | solution.py:55
  8.6 334.2 %reduce-scatter.5.cloned.1.call-start = ((), (), s32[]{:S(2)}) async-start(), calls=%async_computation.6 | async-start | bytes 4718592 | tf_op jit(solution)/shard_map/reduce_scatter | solution.py:62
  127.6 2.5 copy-start.2
  238.7 210.9 %reduce-scatter.7.cloned.1.call-start = ((), (), s32[]{:S(2)}) async-start(), calls=%async_computation.7 | async-start | bytes 8912896 | tf_op jit(solution)/shard_map/reduce_scatter | solution.py:63
  238.7 210.8 %copy-start.1 = (bf16[1024,128]{1,0:T(8,128)(2,1)S(1)}, bf16[1024,128]{1,0:T(8,128)(2,1)}, u32[]{:S(2)}) copy-start(bf16[1024,128]{1,0:T(8,128)(2,1)} %param.9) | copy-start | bytes 786436
  238.7 210.8 %copy-start.3 = (f32[128]{0:T(128)S(1)}, f32[128]{0:T(128)}, u32[]{:S(2)}) copy-start(f32[128]{0:T(128)} %param.10) | copy-start | bytes 1540
  239.3 312.6 %all-gather.9.cloned.1.call-start = ((), (), s32[]{:S(2)}) async-start(), calls=%async_computation.8 | async-start | bytes 2359296 | tf_op jit(solution)/shard_map/all_gather | solution.py:54
  502.1 111.3 %all-gather.11.cloned.1.call-start = ((), (), s32[]{:S(2)}) async-start(), calls=%async_computation.9 | async-start | bytes 4456448 | tf_op jit(solution)/shard_map/all_gather | solution.py:55
  502.7 330.3 %reduce-scatter.9.cloned.1.call-start = ((), (), s32[]{:S(2)}) async-start(), calls=%async_computation.10 | async-start | bytes 4718592 | tf_op jit(solution)/shard_map/reduce_scatter | solution.py:62
  728.8 210.8 %reduce-scatter.11.cloned.1.call-start = ((), (), s32[]{:S(2)}) async-start(), calls=%async_computation.11 | async-start | bytes 8912896 | tf_op jit(solution)/shard_map/reduce_scatter | solution.py:63
  728.9 210.8 %copy-start = (bf16[1024,128]{1,0:T(8,128)(2,1)S(1)}, bf16[1024,128]{1,0:T(8,128)(2,1)}, u32[]{:S(2)}) copy-start(bf16[1024,128]{1,0:T(8,128)(2,1)} %divide_convert_fusion.1) | copy-start | bytes 786436
Sparse Core Ops, SparseCore 0:
  9.6 52.4 all-gather.4
  64.6 58.7 all-gather.6
  238.8 103.9 reduce-scatter.4
  347.0 102.4 reduce-scatter.6
  502.2 49.5 all-gather.8
  554.7 58.7 all-gather.10
  729.0 103.9 reduce-scatter.8
  837.3 102.2 reduce-scatter.10
